TPU v7x, 32 devices: a whole 2x2x4 slice. The times are simulated.
32 devices in a mesh: brick: 8 (over z, x), spec: 4 (over y, core).
Axes of the slice: x: 2, y: 2, z: 4, core: 2. Of those that a mesh axis runs over, the one named last changes fastest.
Arguments:
- rhs: float32 [4, 16, 256, 256], P('spec', 'brick'), may hold values from -24 to 24
- density: float32 [16, 256, 256], P('brick', 'spec'), may hold values from 0.01 to 0.1
- kappa: float32 [4], P('spec'), may hold values from 0.5 to 4
- block_group: int32 [8, 16], replicated, may hold values from 0 to 31, as said below
Outputs:
- solution: float32 [4, 16, 256, 256], P('spec', 'brick')
- residual: float32 [4, 16, 256, 256], P('spec', 'brick')
Inputs may be any that keep to these rules, and one draw needn't show every extreme that they name: `block_group`: every aggregate id 0 to 31 names at least one block; the blocks of one aggregate share one tile position and lie on consecutive bricks.
All inputs are finite; a program needn't handle non-finite values.
Results may differ from a plain program's by a relative error of at most 0.0003.
Values sent between devices are 32-bit elements; how exact they have to be, the bound alone decides.
A program may use at most 64 MiB of HBM per device.

v0:
```python
import functools

import jax
import jax.numpy as jnp
from jax import lax
from jax.experimental import pallas as pl
from jax.experimental.pallas import tpu as pltpu
from jax.sharding import PartitionSpec as P

TILES = 4
COARSE_SWEEPS = 3
CHUNKS = 16
AHEAD = 16
relax_fine = 0.85
relax_coarse = 0.6
MESH = pl.DeviceIdType.MESH
F32 = jnp.float32
BF16 = jnp.bfloat16


def iota(shape, dim):
    return lax.broadcasted_iota(jnp.int32, shape, dim)


def split(x, parts):
    out = []
    for _ in range(parts):
        piece = x.astype(BF16)
        out.append(piece)
        x = x - piece.astype(F32)
    return out


def dot(a, b):
    return jnp.dot(a, b, preferred_element_type=F32)


def filter_rows(m):
    size = m.shape[0]
    row = iota(m.shape, 0)
    before = jnp.where(row == 0, 0.0, pltpu.roll(m, 1, 0))
    after = jnp.where(row == size - 1, 0.0, pltpu.roll(m, size - 1, 0))
    return m + 0.5 * (before + after)


def filter_lanes(m):
    size = m.shape[1]
    lane = iota(m.shape, 1)
    before = jnp.where(lane == 0, 0.0, pltpu.roll(m, 1, 1))
    after = jnp.where(lane == size - 1, 0.0, pltpu.roll(m, size - 1, 1))
    return m + 0.5 * (before + after)


def stencil(low, mid, high):
    return filter_lanes(filter_rows(mid + 0.5 * (low + high)))


def pair_matrix(fine, coarse):
    return (iota((coarse, fine), 1) // 2 == iota((coarse, fine), 0)).astype(BF16)


def pair_matrix_t(fine, coarse):
    return (iota((fine, coarse), 0) // 2 == iota((fine, coarse), 1)).astype(BF16)


def coarsen_sum(x):
    rows, cols = x.shape
    left = pair_matrix(rows, rows // 2)
    right = pair_matrix_t(cols, cols // 2)
    halves = sum(dot(left, piece) for piece in split(x, 2))
    return sum(dot(piece, right) for piece in split(halves, 2)) * 0.125


def refine_layer(c):
    rows, cols = c.shape
    left = pair_matrix_t(2 * rows, rows)
    right = pair_matrix(2 * cols, cols)
    total = None
    for piece in split(c, 2):
        term = dot(dot(left, piece).astype(BF16), right)
        total = term if total is None else total + term
    return total


def kernel(
    n, spec, kappa_hbm, bg_hbm, rhs_ref, dens_ref, sol_ref, res_ref,
    kappa_ref, bg_ref,
    R, D, I, V1, V, S, CR, DC, CI, CA, CB, RS, DSUM, FX,
    prs, prr, frs, frr, dss, dsr, gss, gsr,
    azs, aps, ar, ass, asr, bzs, bps, br, vs, vr, ls,
):
    me = lax.axis_index("brick")
    j = lax.axis_index("spec")
    odd = lax.rem(me, 2)
    partner = me + 1 - 2 * odd
    ny, nz = rhs_ref.shape[1], rhs_ref.shape[2]
    hy, hz = ny // 2, nz // 2
    rows = dens_ref.shape[1]
    half = n // 2
    pslot = 2 - 2 * odd
    fslot = 2 * odd
    fdest = me + 2 - 4 * odd
    fsends = jnp.logical_and(fdest >= 0, fdest < n)
    fsource = me - 2 + 4 * odd
    frecvs = jnp.logical_and(fsource >= 0, fsource < n)
    fdest_c = lax.rem(fdest + n, n)
    fsource_c = lax.rem(fsource + n, n)
    core = j + 1 - 2 * lax.rem(j, 2)
    far = lax.rem(j + spec // 2, spec)
    chunk = ny // CHUNKS

    def remote(src, dst, ssem, rsem, b, s):
        return pltpu.make_async_remote_copy(
            src_ref=src, dst_ref=dst, send_sem=ssem, recv_sem=rsem,
            device_id={"brick": b, "spec": s}, device_id_type=MESH,
        )

    barrier = pltpu.get_barrier_semaphore()
    for k in range(1, half):
        pl.semaphore_signal(barrier, inc=1, device_id={"brick": lax.rem(me + 2 * k, n), "spec": j}, device_id_type=MESH)
    pl.semaphore_signal(barrier, inc=1, device_id={"brick": partner, "spec": j}, device_id_type=MESH)
    pl.semaphore_signal(barrier, inc=1, device_id={"brick": me, "spec": core}, device_id_type=MESH)
    pl.semaphore_signal(barrier, inc=1, device_id={"brick": me, "spec": far}, device_id_type=MESH)

    my_rows = pl.ds(pl.multiple_of(j * rows, 8), rows)
    core_rows = pl.ds(pl.multiple_of(core * rows, 8), rows)
    far_rows = pl.ds(pl.multiple_of(far * rows, 8), rows)
    far_core = lax.rem(core + spec // 2, spec)
    far_core_rows = pl.ds(pl.multiple_of(far_core * rows, 8), rows)
    loads = [
        pltpu.make_async_copy(dens_ref, D.at[1, :, my_rows, :], ls.at[0]),
        pltpu.make_async_copy(kappa_hbm, kappa_ref, ls.at[1]),
        pltpu.make_async_copy(bg_hbm, bg_ref, ls.at[2]),
        pltpu.make_async_copy(rhs_ref, R.at[1], ls.at[3]),
    ]
    for load in loads:
        load.start()
    crows = rows // 2
    cmine = pl.ds(pl.multiple_of(j * crows, 8), crows)
    ccore = pl.ds(pl.multiple_of(core * crows, 8), crows)
    cfar = pl.ds(pl.multiple_of(far * crows, 8), crows)
    cfarcore = pl.ds(pl.multiple_of(far_core * crows, 8), crows)

    V1[0] = jnp.zeros((ny, nz), F32)
    V1[7] = jnp.zeros((ny, nz), F32)
    zero = jnp.zeros((hy, hz), F32)
    for buf in (CA, CB):
        buf[0] = zero
        buf[n + 1] = zero
    for load in loads:
        load.wait()
    kap = kappa_ref[0]
    kap1 = 0.25 * kap
    DC[me, cmine, :] = coarsen_sum(D[1, 0, my_rows, :] + D[1, 1, my_rows, :])
    pl.semaphore_wait(barrier, half - 1 + 3)

    dslot = 2 * odd
    dpair = remote(dens_ref, D.at[dslot, :, my_rows, :], dss.at[0], dsr.at[0], partner, j)
    dpair.start()
    dpair_in = remote(dens_ref, D.at[pslot, :, my_rows, :], dss.at[0], dsr.at[0], partner, j)

    def rchunk(c):
        return pl.ds(pl.multiple_of(c * chunk, 8), chunk)

    def rpair(c, slot):
        return remote(rhs_ref.at[:, rchunk(c), :], R.at[slot, :, rchunk(c), :], prs.at[c], prr.at[c], partner, j)

    def rfwd(c, slot, dest):
        return remote(R.at[pslot, :, rchunk(c), :], R.at[slot, :, rchunk(c), :], frs.at[c], frr.at[c], dest, j)

    slots = (1, pslot, fslot)

    def dsrc(kind):
        return dens_ref if kind == 0 else D.at[slots[kind], :, my_rows, :]

    def dfar(kind, at):
        return remote(dsrc(kind), D.at[slots[kind], :, at, :], gss.at[kind, 0], gsr.at[kind, 0], me, far)

    def dcore(kind, at):
        return remote(dsrc(kind), D.at[slots[kind], :, at, :], gss.at[kind, 1], gsr.at[kind, 1], me, core)

    def dcorefar(kind, at):
        return remote(D.at[slots[kind], :, far_rows, :], D.at[slots[kind], :, at, :], gss.at[kind, 2], gsr.at[kind, 2], me, core)

    dfar(0, my_rows).start()
    dcore(0, my_rows).start()

    def gather_start(view, zs, ps, rs):
        for k in range(1, half):
            remote(view(me), view(me), zs.at[k], rs.at[me], lax.rem(me + 2 * k, n), j).start()
        remote(view(me), view(me), ps.at[0], rs.at[me], partner, j).start()

    def gather_forward(view, zs, ps, rs):
        for k in range(1, half):
            b = lax.rem(me + 2 * k, n)
            remote(view(b), view(b), zs.at[k], rs.at[b], partner, j).wait_recv()
            remote(view(b), view(b), ps.at[k], rs.at[b], partner, j).start()

    def gather_finish(view, zs, ps, rs):
        for k in range(half):
            b = lax.rem(partner + 2 * k, n)
            remote(view(b), view(b), ps.at[k], rs.at[b], partner, j).wait_recv()

    def gather_sent(view, zs, ps, rs):
        for k in range(1, half):
            remote(view(me), view(me), zs.at[k], rs.at[me], partner, j).wait_send()
        for k in range(half):
            remote(view(me), view(me), ps.at[k], rs.at[me], partner, j).wait_send()

    dview = lambda b: DC.at[b, cmine, :]
    dgather = (dview, azs, aps, ar)
    gather_start(*dgather)
    for c in range(AHEAD):
        rpair(c, dslot).start()

    def cfar_copy(at):
        return remote(DC.at[:, cmine, :], DC.at[:, at, :], ass.at[0], asr.at[0], me, far)

    def ccore_copy(at):
        return remote(DC.at[:, cmine, :], DC.at[:, at, :], ass.at[1], asr.at[1], me, core)

    def ccorefar_copy(at):
        return remote(DC.at[:, cfar, :], DC.at[:, at, :], ass.at[2], asr.at[2], me, core)

    dpair_in.wait_recv()

    def dfwd(slot, dest):
        return remote(D.at[pslot, :, my_rows, :], D.at[slot, :, my_rows, :], dss.at[1], dsr.at[1], dest, j)

    @pl.when(fsends)
    def _():
        dfwd(2 * odd, fdest_c).start()

    dfar(1, my_rows).start()
    dcore(1, my_rows).start()

    def gather_forward_one(view, zs, ps, rs, k):
        b = lax.rem(me + 2 * k, n)
        remote(view(b), view(b), zs.at[k], rs.at[b], partner, j).wait_recv()
        remote(view(b), view(b), ps.at[k], rs.at[b], partner, j).start()

    for c in range(CHUNKS):
        rpair(c, pslot).wait_recv()
        if c + AHEAD < CHUNKS:
            rpair(c + AHEAD, dslot).start()

        @pl.when(fsends)
        def _():
            rfwd(c, 2 * odd, fdest_c).start()

        if c == 1:
            dfar(0, far_rows).wait_recv()
            dcorefar(0, far_rows).start()
            gather_forward(*dgather)
        if c == 1:
            dfar(1, far_rows).wait_recv()
            dcorefar(1, far_rows).start()

            @pl.when(frecvs)
            def _():
                dfwd(fslot, fsource_c).wait_recv()
                dfar(2, my_rows).start()
                dcore(2, my_rows).start()

        if c == CHUNKS - 1:
            gather_finish(*dgather)
            cfar_copy(cmine).start()
            ccore_copy(cmine).start()
        if c == 11:
            @pl.when(frecvs)
            def _():
                dfar(2, far_rows).wait_recv()
                dcorefar(2, far_rows).start()


    def prepare(slot, valid):
        def body(i, carry):
            inv = relax_fine / (D[slot, i] + 14.0 * kap)
            I[slot, i] = inv
            first = R[slot, i] * inv
            V1[2 * slot + i + 1] = first if valid is None else jnp.where(valid, first, 0.0)
            return carry

        lax.fori_loop(0, 2, body, 0)

    dcore(0, core_rows).wait_recv()
    dcorefar(0, far_core_rows).wait_recv()
    prepare(1, None)
    dcore(1, core_rows).wait_recv()
    dcorefar(1, far_core_rows).wait_recv()
    prepare(pslot, None)

    def inside(e):
        g = 2 * me + e - 3
        return jnp.logical_and(g >= 0, g < 2 * n)

    def relax_layer(src, e):
        slot, i = (e - 1) // 2, lax.rem(e - 1, 2)
        v = src[e]
        f = stencil(src[e - 1], v, src[e + 1])
        out = (1.0 - relax_fine) * v + I[slot, i] * (R[slot, i] + 2.0 * kap * (f - v))
        return jnp.where(inside(e), out, 0.0)

    def residual_layer(src, e):
        i = e - 3
        v = src[e]
        f = stencil(src[e - 1], v, src[e + 1])
        return R[1, i] - (D[1, i] + 16.0 * kap) * v + 2.0 * kap * f

    base = 4 - 2 * odd
    other = 2 + 2 * odd

    def vout(i):
        return remote(V.at[base + i], V.at[6 * odd + i], vs.at[0, i], vr.at[0, i], fdest_c, j)

    def vback(i):
        return remote(V.at[other + i], V.at[6 - 6 * odd + i], vs.at[1, i], vr.at[1, i], fsource_c, j)

    def vout_in(i):
        return remote(V.at[base + i], V.at[6 * odd + i], vs.at[0, i], vr.at[0, i], fsource_c, j)

    def vback_in(i):
        return remote(V.at[other + i], V.at[6 - 6 * odd + i], vs.at[1, i], vr.at[1, i], fdest_c, j)

    def second(e):
        V[e] = relax_layer(V1, e)

    second(base)

    second(base + 1)

    @pl.when(frecvs)
    def _():
        dcore(2, core_rows).wait_recv()
        dcorefar(2, far_core_rows).wait_recv()
        for c in range(CHUNKS):
            rfwd(c, fslot, fsource_c).wait_recv()
        prepare(fslot, None)

    @pl.when(jnp.logical_not(frecvs))
    def _():
        for i in range(2):
            V1[2 * fslot + i + 1] = jnp.zeros((ny, nz), F32)

    second(other)
    second(other + 1)
    CR[me] = coarsen_sum(residual_layer(V, 3) + residual_layer(V, 4))
    rview = lambda b: CR.at[b]
    rgather = (rview, bzs, bps, br)
    gather_start(*rgather)

    @pl.when(fsends)
    def _():
        vout(0).start()
        vout(1).start()

    @pl.when(frecvs)
    def _():
        vback(0).start()
        vback(1).start()

    cfar_copy(cfar).wait_recv()
    ccorefar_copy(cfar).start()
    gather_forward(*rgather)
    ccore_copy(ccore).wait_recv()
    ccorefar_copy(cfarcore).wait_recv()

    edge = hy // TILES
    lane_tile = iota((hz, hz), 0) // (hz // TILES) == iota((hz, hz), 1) // (hz // TILES)
    same_tile = lane_tile.astype(BF16)

    def lane_sums(x):
        return sum(dot(piece, same_tile) for piece in split(x, 3))

    bgf = bg_ref[...].astype(F32).astype(BF16)
    ids = []
    for ty in range(TILES):
        pick = iota((TILES * TILES, hz), 0) == ty * TILES + iota((TILES * TILES, hz), 1) // (hz // TILES)
        ids.append(dot(bgf, pick.astype(BF16)))

    brick_row = iota((n, hz), 0)
    lane = iota((n, hz), 1)
    tile_lanes = hz // TILES

    def lower_brick(x, fill):
        return jnp.where(brick_row == 0, fill, pltpu.roll(x, 1, 0))

    def upper_brick(x, fill):
        return jnp.where(brick_row == n - 1, fill, pltpu.roll(x, n - 1, 0))

    def group_sums(fields):
        out = []
        for ty in range(TILES):
            total = jnp.zeros((n, hz), F32)
            for b in range(n):
                total = total + jnp.where(ids[ty][b : b + 1] == ids[ty], fields[ty][b : b + 1], 0.0)
            out.append(total)
        return out

    def coarse_first(b, carry):
        d = DC[b]
        CI[b] = relax_fine / (d + 14.0 * kap1)
        for ty in range(TILES):
            DSUM[ty, pl.ds(b, 1), :] = jnp.sum(d[ty * edge : (ty + 1) * edge], axis=0, keepdims=True)
        return carry

    lax.fori_loop(0, n, coarse_first, 0)
    dens_sum = [lane_sums(DSUM[ty]) for ty in range(TILES)]
    weight = []
    for ty in range(TILES):
        fx = 1.0 + 0.5 * (lower_brick(ids[ty], -1.0) == ids[ty]).astype(F32)
        fx = fx + 0.5 * (upper_brick(ids[ty], -1.0) == ids[ty]).astype(F32)
        cells = edge * tile_lanes
        weight.append(16.0 * cells - 2.0 * (2 * edge - 1) * (2 * tile_lanes - 1) * fx)
    totals0 = group_sums(dens_sum)
    totals1 = group_sums(weight)
    step = [relax_coarse / (totals0[ty] + kap1 * totals1[ty]) for ty in range(TILES)]

    @pl.when(me == 1)
    def _():
        V[1] = relax_layer(V1, 1)
        V[0] = jnp.zeros((ny, nz), F32)

    @pl.when(me == 0)
    def _():
        V[0] = jnp.zeros((ny, nz), F32)
        V[1] = jnp.zeros((ny, nz), F32)

    @pl.when(me == n - 2)
    def _():
        V[6] = relax_layer(V1, 6)
        V[7] = jnp.zeros((ny, nz), F32)

    @pl.when(me == n - 1)
    def _():
        V[6] = jnp.zeros((ny, nz), F32)
        V[7] = jnp.zeros((ny, nz), F32)

    gather_finish(*rgather)

    def coarse_start(b, carry):
        CA[b + 1] = CR[b] * CI[b]
        return carry

    lax.fori_loop(0, n, coarse_start, 0)

    def coarse_defect(src, b):
        v = src[b + 1]
        f = stencil(src[b], v, src[b + 2])
        return v, CR[b] - (DC[b] + 16.0 * kap1) * v + 2.0 * kap1 * f

    def coarse_relax(src, dst):
        def body(b, carry):
            v = src[b + 1]
            f = stencil(src[b], v, src[b + 2])
            dst[b + 1] = (1.0 - relax_fine) * v + CI[b] * (CR[b] + 2.0 * kap1 * (f - v))
            return carry

        return body

    lax.fori_loop(0, n, coarse_relax(CA, CB), 0)

    def remainder(b, carry):
        defect = coarse_defect(CB, b)[1]
        for ty in range(TILES):
            RS[ty, pl.ds(b, 1), :] = jnp.sum(defect[ty * edge : (ty + 1) * edge], axis=0, keepdims=True)
        return carry

    lax.fori_loop(0, n, remainder, 0)
    group_rhs = group_sums([lane_sums(RS[ty]) for ty in range(TILES)])
    fix = [step[ty] * group_rhs[ty] for ty in range(TILES)]

    def aggregate_image(g):
        along = [x + 0.5 * (lower_brick(x, 0.0) + upper_brick(x, 0.0)) for x in g]
        blank = jnp.zeros((n, hz), F32)
        out = []
        for ty in range(TILES):
            below = along[ty - 1] if ty > 0 else blank
            above = along[ty + 1] if ty < TILES - 1 else blank
            mid = (2.0 * edge - 1.0) * along[ty] + 0.5 * (below + above)
            left = jnp.where(lane < tile_lanes, 0.0, pltpu.roll(mid, tile_lanes, 1))
            right = jnp.where(lane >= hz - tile_lanes, 0.0, pltpu.roll(mid, hz - tile_lanes, 1))
            f = (2.0 * tile_lanes - 1.0) * mid + 0.5 * (left + right)
            own = dens_sum[ty] + 16.0 * kap1 * (edge * tile_lanes)
            out.append(own * g[ty] - 2.0 * kap1 * f)
        return group_sums(out)

    for _ in range(COARSE_SWEEPS - 1):
        image = aggregate_image(fix)
        fix = [fix[ty] + step[ty] * (group_rhs[ty] - image[ty]) for ty in range(TILES)]
    for ty in range(TILES):
        FX[ty] = fix[ty]

    def add_fix(b, carry):
        for ty in range(TILES):
            part = pl.ds(ty * edge, edge)
            CA[b + 1, part, :] = CB[b + 1, part, :] + FX[ty, pl.ds(b, 1), :]
        return carry

    def near(width):
        return jnp.maximum(me - width, 0), jnp.minimum(me + width + 1, n)

    lax.fori_loop(*near(4), add_fix, 0)
    lax.fori_loop(*near(3), coarse_relax(CA, CB), 0)
    lax.fori_loop(*near(2), coarse_relax(CB, CA), 0)

    def inner(t, carry):
        b = me + t - 2
        valid = jnp.logical_and(b >= 0, b < n)
        fine = refine_layer(CA[jnp.clip(b, 0, n - 1) + 1])
        for e, add in ((2 * t - 1, t > 1), (2 * t, t < 3)):
            S[e] = jnp.where(valid, V[e] + fine if add else fine, 0.0)
        return carry

    for t in (1, 2, 3):
        inner(t, 0)
    for t, e in ((0, 0), (4, 7)):
        b = me + t - 2
        valid = jnp.logical_and(b >= 0, b < n)
        S[e] = jnp.where(valid, refine_layer(CA[jnp.clip(b, 0, n - 1) + 1]), 0.0)

    def third(e, carry):
        V1[e] = relax_layer(S, e)
        return carry

    lax.fori_loop(3, 5, third, 0)

    @pl.when(frecvs)
    def _():
        vout_in(0).wait_recv()
        vout_in(1).wait_recv()

    @pl.when(fsends)
    def _():
        vback_in(0).wait_recv()
        vback_in(1).wait_recv()

    for e in (0, 1, 6, 7):
        S[e] = jnp.where(inside(e), S[e] + V[e], 0.0)
    lax.fori_loop(1, 3, third, 0)
    lax.fori_loop(5, 7, third, 0)

    def fourth(e, carry):
        S[e] = relax_layer(V1, e)
        return carry

    lax.fori_loop(2, 6, fourth, 0)

    def last(i, carry):
        sol_ref[i] = S[i + 3]
        res_ref[i] = residual_layer(S, i + 3)
        return carry

    lax.fori_loop(0, 2, last, 0)

    dpair.wait_send()
    for c in range(CHUNKS):
        rpair(c, dslot).wait_send()
    for kind in (0, 1):
        dfar(kind, my_rows).wait_send()
        dcore(kind, my_rows).wait_send()
        dcorefar(kind, far_rows).wait_send()

    @pl.when(frecvs)
    def _():
        dfar(2, my_rows).wait_send()
        dcore(2, my_rows).wait_send()
        dcorefar(2, far_rows).wait_send()

    @pl.when(fsends)
    def _():
        dfwd(2 * odd, fdest_c).wait_send()
        for c in range(CHUNKS):
            rfwd(c, 2 * odd, fdest_c).wait_send()

    gather_sent(*dgather)
    gather_sent(*rgather)
    cfar_copy(cmine).wait_send()
    ccore_copy(cmine).wait_send()
    ccorefar_copy(cfar).wait_send()

    @pl.when(fsends)
    def _():
        vout(0).wait_send()
        vout(1).wait_send()

    @pl.when(frecvs)
    def _():
        vback(0).wait_send()
        vback(1).wait_send()


def local(n, spec, rhs, density, kappa, block_group):
    _, cells, ny, nz = rhs.shape
    hy, hz = ny // 2, nz // 2
    fine = lambda *lead: pltpu.VMEM(lead + (ny, nz), F32)
    coarse = lambda *lead: pltpu.VMEM(lead + (hy, hz), F32)
    dma = lambda *shape: pltpu.SemaphoreType.DMA(shape)
    vmem = pl.BlockSpec(memory_space=pltpu.VMEM)
    out = jax.ShapeDtypeStruct((cells, ny, nz), F32)
    sol, res = pl.pallas_call(
        functools.partial(kernel, n, spec),
        out_shape=(out, out),
        in_specs=[pl.BlockSpec(memory_space=pltpu.HBM)] * 4,
        out_specs=(vmem, vmem),
        scratch_shapes=[
            pltpu.SMEM((1,), F32), pltpu.VMEM(block_group.shape, jnp.int32),
            fine(3, 2), fine(3, 2), fine(3, 2), fine(8), fine(8), fine(8),
            coarse(n), coarse(n), coarse(n), coarse(n + 2), coarse(n + 2),
            pltpu.VMEM((TILES, n, hz), F32), pltpu.VMEM((TILES, n, hz), F32), pltpu.VMEM((TILES, n, hz), F32),
            dma(CHUNKS), dma(CHUNKS), dma(CHUNKS), dma(CHUNKS), dma(2), dma(2), dma(3, 3), dma(3, 3),
            dma(n // 2), dma(n // 2), dma(n), dma(3), dma(3),
            dma(n // 2), dma(n // 2), dma(n), dma(2, 2), dma(2, 2), dma(4),
        ],
        compiler_params=pltpu.CompilerParams(
            collective_id=0, has_side_effects=True, vmem_limit_bytes=(20 << 20) + 24 * n * hy * hz
        ),
    )(kappa, block_group, rhs.reshape(cells, ny, nz), density)
    return sol[None], res[None]


def solution(mesh):
    return jax.shard_map(
        functools.partial(local, mesh.shape["brick"], mesh.shape["spec"]),
        mesh=mesh,
        in_specs=(P("spec", "brick", None, None), P("brick", "spec", None), P("spec"), P()),
        out_specs=(P("spec", "brick", None, None), P("spec", "brick", None, None)),
        check_vma=False,
    )
```

profile of v0, /device:TPU:0, one launch (start us, length us, event | category | flops | bytes accessed | tf_op | source)
XLA Modules:
  0.0 52.1 jit_solution(15283132489228916789)
XLA Ops:
  1.3 0.0 copy-start
  1.3 1.0 %copy-done = f32[1,2,256,256]{3,2,1,0:T(8,128)S(1)} copy-done((f32[1,2,256,256]{3,2,1,0:T(8,128)S(1)}, f32[1,2,256,256]{3,2,1,0:T(8,128)}, u32[]{:S(2)}) %copy-start) | copy-done | bytes 524312
  2.3 0.0 copy-start.1
  2.3 0.9 %copy-done.1 = f32[2,64,256]{2,1,0:T(8,128)S(1)} copy-done((f32[2,64,256]{2,1,0:T(8,128)S(1)}, f32[2,64,256]{2,1,0:T(8,128)}, u32[]{:S(2)}) %copy-start.1) | copy-done | bytes 131096
  3.2 0.0 copy-start.2
  3.2 0.7 %copy-done.2 = s32[8,16]{1,0:T(8,128)S(1)} copy-done((s32[8,16]{1,0:T(8,128)S(1)}, s32[8,16]{1,0:T(8,128)}, u32[]{:S(2)}) %copy-start.2) | copy-done | bytes 536
  3.9 46.6 %shard_map.59 = (f32[2,256,256]{2,1,0:T(8,128)S(1)}, f32[2,256,256]{2,1,0:T(8,128)S(1)}) custom-call(f32[1]{0:T(128)S(6)} %copy.8.kappa_hbm, s32[8,16]{1,0:T(8,128)S(1)} %copy-done.2, f32[2,256,256]{2,1,0:T(8,128)S(1)} %bitcast.3, f32[2,64,256]{2,1,0:T(8,128)S(1)} %copy-done.1), custom_call_target="tpu_custom_call" | custom-call | tf_op jit(solution)/shard_map/pallas_call | solution.py:601
  50.5 0.8 %copy.9 = f32[1,2,256,256]{3,2,1,0:T(8,128)} copy(f32[1,2,256,256]{3,2,1,0:T(8,128)S(1)} %bitcast.5) | data formatting | bytes 1048576
  51.3 0.8 %copy.10 = f32[1,2,256,256]{3,2,1,0:T(8,128)} copy(f32[1,2,256,256]{3,2,1,0:T(8,128)S(1)} %bitcast.4) | data formatting | bytes 1048576
Async XLA Ops:
  1.3 1.0 %copy-start = (f32[1,2,256,256]{3,2,1,0:T(8,128)S(1)}, f32[1,2,256,256]{3,2,1,0:T(8,128)}, u32[]{:S(2)}) copy-start(f32[1,2,256,256]{3,2,1,0:T(8,128)} %param.4) | copy-start | bytes 1572868
  2.3 0.9 %copy-start.1 = (f32[2,64,256]{2,1,0:T(8,128)S(1)}, f32[2,64,256]{2,1,0:T(8,128)}, u32[]{:S(2)}) copy-start(f32[2,64,256]{2,1,0:T(8,128)} %dens_ref.1) | copy-start | bytes 393220
  3.2 0.7 %copy-start.2 = (s32[8,16]{1,0:T(8,128)S(1)}, s32[8,16]{1,0:T(8,128)}, u32[]{:S(2)}) copy-start(s32[8,16]{1,0:T(8,128)} %bg_hbm.1) | copy-start | bytes 1540
where the time goes:
time: 52.3 us; the launch traced here: 52.1 us
  Pallas kernels  46.6 us (89%)
  local copies, waits for them, and re-layouts  4.21 us (8%)
  between operations  1.3 us (2%)
    pallas_call x1, Pallas kernels, local(): pl.pallas_call(functools.partial(kernel, n, spec), out_shape=(out, out),...  46.6 us
    unnamed x8, local copies, waits for them, and re-layouts  4.21 us

commit v1 on v0

--- a/solution.py
+++ b/solution.py
@@ -598,6 +598,7 @@
     dma = lambda *shape: pltpu.SemaphoreType.DMA(shape)
     vmem = pl.BlockSpec(memory_space=pltpu.VMEM)
     out = jax.ShapeDtypeStruct((cells, ny, nz), F32)
+    hbm = lambda x: pltpu.with_memory_space_constraint(x, pltpu.HBM)
     sol, res = pl.pallas_call(
         functools.partial(kernel, n, spec),
         out_shape=(out, out),
@@ -615,7 +616,7 @@
         compiler_params=pltpu.CompilerParams(
             collective_id=0, has_side_effects=True, vmem_limit_bytes=(20 << 20) + 24 * n * hy * hz
         ),
-    )(kappa, block_group, rhs.reshape(cells, ny, nz), density)
+    )(kappa, hbm(block_group), hbm(rhs.reshape(cells, ny, nz)), hbm(density))
     return sol[None], res[None]
 
 

time: 52.3 us -> 49.9 us (0.954)
  local copies, waits for them, and re-layouts: 4.21 us -> 1.59 us
    unnamed x8 -> x2, local copies, waits for them, and re-layouts: 4.21 us -> 1.59 us
where the time goes in v1:
time: 49.9 us; the launch traced here: 49.8 us
  Pallas kernels  46.9 us (94%)
  local copies, waits for them, and re-layouts  1.59 us (3%)
  between operations  1.28 us (3%)
    pallas_call x1, Pallas kernels, local(): pl.pallas_call(functools.partial(kernel, n, spec), out_shape=(out, out),...  46.9 us
    unnamed x2, local copies, waits for them, and re-layouts  1.59 us

profile of v1, /device:TPU:0, one launch (start us, length us, event | category | flops | bytes accessed | tf_op | source)
XLA Modules:
  0.0 49.8 jit_solution(14157152559977217300)
XLA Ops:
  1.3 46.9 %shard_map.59 = (f32[2,256,256]{2,1,0:T(8,128)S(1)}, f32[2,256,256]{2,1,0:T(8,128)S(1)}) custom-call(f32[1]{0:T(128)S(6)} %copy.8.kappa_hbm, s32[8,16]{1,0:T(8,128)} %bg_hbm.1, f32[2,256,256]{2,1,0:T(8,128)} %bitcast.5, f32[2,64,256]{2,1,0:T(8,128)} %dens_ref.1), custom_call_target="tpu_custom_call" | custom-call | tf_op jit(solution)/shard_map/pallas_call | solution.py:602
  48.2 0.8 %copy.9 = f32[1,2,256,256]{3,2,1,0:T(8,128)} copy(f32[1,2,256,256]{3,2,1,0:T(8,128)S(1)} %bitcast.4) | data formatting | bytes 1048576
  49.0 0.8 %copy.10 = f32[1,2,256,256]{3,2,1,0:T(8,128)} copy(f32[1,2,256,256]{3,2,1,0:T(8,128)S(1)} %bitcast.3) | data formatting | bytes 1048576

commit v2 on v1

v2 whole, which is shorter than its diff:
```python
import functools

import jax
import jax.numpy as jnp
from jax import lax
from jax.experimental import pallas as pl
from jax.experimental.pallas import tpu as pltpu
from jax.sharding import PartitionSpec as P

TILES = 4
COARSE_SWEEPS = 3
relax_fine = 0.85
relax_coarse = 0.6
MESH = pl.DeviceIdType.MESH
F32 = jnp.float32
BF16 = jnp.bfloat16


def iota(shape, dim):
    return lax.broadcasted_iota(jnp.int32, shape, dim)


def split(x, parts):
    out = []
    for _ in range(parts):
        piece = x.astype(BF16)
        out.append(piece)
        x = x - piece.astype(F32)
    return out


def dot(a, b):
    return jnp.dot(a, b, preferred_element_type=F32)


def filter_rows(m):
    size = m.shape[0]
    row = iota(m.shape, 0)
    before = jnp.where(row == 0, 0.0, pltpu.roll(m, 1, 0))
    after = jnp.where(row == size - 1, 0.0, pltpu.roll(m, size - 1, 0))
    return m + 0.5 * (before + after)


def filter_lanes(m):
    size = m.shape[1]
    lane = iota(m.shape, 1)
    before = jnp.where(lane == 0, 0.0, pltpu.roll(m, 1, 1))
    after = jnp.where(lane == size - 1, 0.0, pltpu.roll(m, size - 1, 1))
    return m + 0.5 * (before + after)


def stencil(low, mid, high):
    return filter_lanes(filter_rows(mid + 0.5 * (low + high)))


def pair_matrix(fine, coarse):
    return (iota((coarse, fine), 1) // 2 == iota((coarse, fine), 0)).astype(BF16)


def pair_matrix_t(fine, coarse):
    return (iota((fine, coarse), 0) // 2 == iota((fine, coarse), 1)).astype(BF16)


def coarsen_sum(x, left=None):
    rows, cols = x.shape
    if left is None:
        left = pair_matrix(rows, rows // 2)
    right = pair_matrix_t(cols, cols // 2)
    halves = sum(dot(left, piece) for piece in split(x, 2))
    return sum(dot(piece, right) for piece in split(halves, 2)) * 0.125


def pieces_of(rows):
    units = rows // 8
    sizes = [max(1, round(units * share)) for share in (0.3, 0.3, 0.22, 0.12)]
    sizes.append(units - sum(sizes))
    starts = [sum(sizes[:c]) for c in range(len(sizes))]
    return [(8 * start, 8 * size) for start, size in zip(starts, sizes)]


def refine_layer(c):
    rows, cols = c.shape
    left = pair_matrix_t(2 * rows, rows)
    right = pair_matrix(2 * cols, cols)
    total = None
    for piece in split(c, 2):
        term = dot(dot(left, piece).astype(BF16), right)
        total = term if total is None else total + term
    return total


def kernel(
    n, spec, kappa_hbm, bg_hbm, rhs_ref, dens_ref, sol_ref, res_ref,
    kappa_ref, bg_ref,
    R, RF, D, IW, IE, V1, V2, W3, W4, WX, S, E3, CR, DC, CI, CA, CB, RS, DSUM, FX,
    prs, prr, frs, frr, rgs, rgr, dss, dsr, gss, gsr, dgs, dgr,
    azs, aps, ar, ass, asr, bzs, bps, br, w3s, w3r, w4s, w4r, xs, xr, ls,
):
    me = lax.axis_index("brick")
    j = lax.axis_index("spec")
    odd = lax.rem(me, 2)
    even = 1 - odd
    base = me - odd
    partner = base + even
    ny, nz = rhs_ref.shape[1], rhs_ref.shape[2]
    hy, hz = ny // 2, nz // 2
    rows = dens_ref.shape[1]
    half = n // 2
    window = R.shape[1]
    pieces = pieces_of(window)
    down, up = base > 0, base + 2 < n
    flow = jnp.logical_or(jnp.logical_and(odd == 0, down), jnp.logical_and(odd == 1, up))
    fhigh = jnp.logical_or(jnp.logical_and(odd == 0, up), jnp.logical_and(odd == 1, down))
    onward = lax.rem(me + 2 - 4 * odd + n, n)
    back = lax.rem(me - 2 + 4 * odd + n, n)
    below = lax.rem(me - 2 + n, n)
    above = lax.rem(me + 2, n)
    core = j + 1 - 2 * lax.rem(j, 2)
    far = lax.rem(j + spec // 2, spec)
    mine, theirs, near_slot, far_slot = 1 + odd, 2 - odd, 3 * odd, 3 - 3 * odd

    def remote(src, dst, ssem, rsem, b, s):
        return pltpu.make_async_remote_copy(
            src_ref=src, dst_ref=dst, send_sem=ssem, recv_sem=rsem,
            device_id={"brick": b, "spec": s}, device_id_type=MESH,
        )

    barrier = pltpu.get_barrier_semaphore()
    for k in range(1, half):
        pl.semaphore_signal(barrier, inc=1, device_id={"brick": lax.rem(me + 2 * k, n), "spec": j}, device_id_type=MESH)
    pl.semaphore_signal(barrier, inc=1, device_id={"brick": partner, "spec": j}, device_id_type=MESH)
    pl.semaphore_signal(barrier, inc=1, device_id={"brick": me, "spec": core}, device_id_type=MESH)
    pl.semaphore_signal(barrier, inc=1, device_id={"brick": me, "spec": far}, device_id_type=MESH)

    def eight(start, size):
        return pl.ds(pl.multiple_of(start, 8), size)

    far_core = lax.rem(core + spec // 2, spec)
    my_rows, core_rows, far_rows, far_core_rows = [eight(at * rows, rows) for at in (j, core, far, far_core)]
    crows = rows // 2
    cmine, ccore, cfar, cfarcore = [eight(at * crows, crows) for at in (j, core, far, far_core)]
    win = odd * (ny - window)
    their_win = even * (ny - window)
    lead = 8 * odd
    my_half, their_half = eight(odd * hy, hy), eight(even * hy, hy)
    loads = [
        pltpu.make_async_copy(dens_ref, D.at[mine, :, my_rows, :], ls.at[0]),
        pltpu.make_async_copy(kappa_hbm, kappa_ref, ls.at[1]),
        pltpu.make_async_copy(bg_hbm, bg_ref, ls.at[2]),
        pltpu.make_async_copy(rhs_ref.at[:, eight(win, window), :], R.at[pl.ds(2 * mine, 2)], ls.at[3]),
        pltpu.make_async_copy(rhs_ref, RF, ls.at[4]),
    ]
    for load in loads:
        load.start()

    blank = jnp.zeros((window, nz), F32)

    @pl.when(jnp.logical_not(down))
    def _():
        for buf, q in ((V1, 0), (V1, 1), (V2, 1), (W3, 1), (W4, 1)):
            buf[q] = blank

    @pl.when(jnp.logical_not(up))
    def _():
        for buf, q in ((V1, 6), (V1, 7), (V2, 6), (W3, 6), (W4, 6)):
            buf[q] = blank

    zero = jnp.zeros((hy, hz), F32)
    for buf in (CA, CB):
        buf[0] = zero
        buf[n + 1] = zero
    for load in loads[:3]:
        load.wait()
    kap = kappa_ref[0]
    kap1 = 0.25 * kap
    DC[me, cmine, :] = coarsen_sum(D[mine, 0, my_rows, :] + D[mine, 1, my_rows, :])
    pl.semaphore_wait(barrier, half - 1 + 3)

    def dpair(i, slot):
        return remote(dens_ref.at[i], D.at[slot, i, my_rows, :], dss.at[0, i], dsr.at[0, i], partner, j)

    def dfwd(i, dest):
        return remote(D.at[theirs, i, my_rows, :], D.at[near_slot, i, my_rows, :], dss.at[1, i], dsr.at[1, i], dest, j)

    def rpair(c, slot):
        start, size = pieces[c]
        return remote(
            rhs_ref.at[:, eight(their_win + start, size), :], R.at[pl.ds(2 * slot, 2), pl.ds(start, size), :],
            prs.at[c], prr.at[c], partner, j,
        )

    def rfwd(c, dest):
        start, size = pieces[c]
        return remote(
            R.at[pl.ds(2 * theirs, 2), pl.ds(start, size), :], R.at[pl.ds(2 * near_slot, 2), pl.ds(start, size), :],
            frs.at[c], frr.at[c], dest, j,
        )

    def rback(dest):
        return remote(rhs_ref.at[:, eight(win, window), :], R.at[pl.ds(2 * far_slot, 2)], rgs.at[0], rgr.at[0], dest, j)

    slots = (mine, theirs, near_slot)

    def dsrc(kind, i):
        return dens_ref.at[i] if kind == 0 else D.at[slots[kind], i, my_rows, :]

    def dfar(kind, i, at):
        return remote(dsrc(kind, i), D.at[slots[kind], i, at, :], gss.at[kind, 0, i], gsr.at[kind, 0, i], me, far)

    def dcore(kind, i, at):
        return remote(dsrc(kind, i), D.at[slots[kind], i, at, :], gss.at[kind, 1, i], gsr.at[kind, 1, i], me, core)

    def dcorefar(kind, i, at):
        return remote(
            D.at[slots[kind], i, far_rows, :], D.at[slots[kind], i, at, :], gss.at[kind, 2, i], gsr.at[kind, 2, i], me, core
        )

    strip = (hy + 16) // 2
    strip_win = odd * (hy - 16)

    def strip_rows(which):
        return eight(strip_win + strip * which, strip)

    lane_of = lax.rem(j, 2)

    def dback(dest):
        at = strip_rows(lane_of)
        return remote(D.at[mine, :, at, :], D.at[far_slot, :, at, :], dgs.at[0], dgr.at[0], dest, j)

    def dbackcore(which):
        at = strip_rows(which)
        return remote(D.at[far_slot, :, at, :], D.at[far_slot, :, at, :], dgs.at[1], dgr.at[1], me, core)

    def gather_start(view, zs, ps, rs):
        for k in range(1, half):
            remote(view(me), view(me), zs.at[k], rs.at[me], lax.rem(me + 2 * k, n), j).start()
        remote(view(me), view(me), ps.at[0], rs.at[me], partner, j).start()

    def gather_forward(view, zs, ps, rs):
        for k in range(1, half):
            b = lax.rem(me + 2 * k, n)
            remote(view(b), view(b), zs.at[k], rs.at[b], partner, j).wait_recv()
            remote(view(b), view(b), ps.at[k], rs.at[b], partner, j).start()

    def gather_finish(view, zs, ps, rs):
        for k in range(half):
            b = lax.rem(partner + 2 * k, n)
            remote(view(b), view(b), ps.at[k], rs.at[b], partner, j).wait_recv()

    def gather_sent(view, zs, ps, rs):
        for k in range(1, half):
            remote(view(me), view(me), zs.at[k], rs.at[me], partner, j).wait_send()
        for k in range(half):
            remote(view(me), view(me), ps.at[k], rs.at[me], partner, j).wait_send()

    dview = lambda b: DC.at[b, cmine, :]
    dgather = (dview, azs, aps, ar)
    for i in range(2):
        dpair(i, mine).start()
    for i in range(2):
        dfar(0, i, my_rows).start()
        dcore(0, i, my_rows).start()

    @pl.when(flow)
    def _():
        rback(back).start()

    gather_start(*dgather)
    for c in range(len(pieces)):
        rpair(c, mine).start()

    def cfar_copy(at):
        return remote(DC.at[:, cmine, :], DC.at[:, at, :], ass.at[0], asr.at[0], me, far)

    def ccore_copy(at):
        return remote(DC.at[:, cmine, :], DC.at[:, at, :], ass.at[1], asr.at[1], me, core)

    def ccorefar_copy(at):
        return remote(DC.at[:, cfar, :], DC.at[:, at, :], ass.at[2], asr.at[2], me, core)

    for i in range(2):
        dpair(i, theirs).wait_recv()

        @pl.when(fhigh)
        def _():
            dfwd(i, onward).start()

        dfar(1, i, my_rows).start()
        dcore(1, i, my_rows).start()
        dfar(0, i, far_rows).wait_recv()
        dcorefar(0, i, far_rows).start()

    def pass_on(c):
        rpair(c, theirs).wait_recv()

        @pl.when(fhigh)
        def _():
            rfwd(c, onward).start()

    for i in range(2):
        dcore(0, i, core_rows).wait_recv()
        dcorefar(0, i, far_core_rows).wait_recv()

    @pl.when(flow)
    def _():
        dback(back).start()

    pass_on(0)
    pass_on(1)
    gather_forward(*dgather)

    @pl.when(flow)
    def _():
        for i in range(2):
            dfwd(i, back).wait_recv()
            dfar(2, i, my_rows).start()
            dcore(2, i, my_rows).start()

    pass_on(2)
    for i in range(2):
        dfar(1, i, far_rows).wait_recv()
        dcorefar(1, i, far_rows).start()
    for c in range(3, len(pieces)):
        pass_on(c)
    gather_finish(*dgather)
    @pl.when(fhigh)
    def _():
        dback(onward).wait_recv()
        dbackcore(lane_of).start()

    def prepare(slot):
        def body(i, carry):
            inv = relax_fine / (D[slot, i, eight(win, window), :] + 14.0 * kap)
            IW[2 * slot + i] = inv
            V1[2 * slot + i] = R[2 * slot + i] * inv
            return carry

        lax.fori_loop(0, 2, body, 0)

    def layer(k):
        return k + odd * (7 - 2 * k)

    def relax_window(src, dst, q):
        v = src[q]
        f = stencil(src[q - 1], v, src[q + 1])
        dst[q] = (1.0 - relax_fine) * v + IW[q] * (R[q] + 2.0 * kap * (f - v))

    def residual_window(q):
        v = V2[q]
        f = stencil(V2[q - 1], v, V2[q + 1])
        d = D[q // 2, lax.rem(q, 2), eight(win, window), :]
        return R[q] - (d + 16.0 * kap) * v + 2.0 * kap * f

    chalf = hy // 2
    pick = (iota((chalf, window), 1) // 2 - lead // 2 == iota((chalf, window), 0)).astype(BF16)

    def coarse_rows_of(parity):
        return eight(parity * chalf, chalf)

    def restrict(q, brick):
        CR[brick, coarse_rows_of(odd), :] = coarsen_sum(residual_window(q) + residual_window(q + 1), pick)

    loads[3].wait()
    loads[4].wait()
    prepare(mine)

    @pl.when(flow)
    def _():
        for i in range(2):
            dfar(2, i, far_rows).wait_recv()
            dcorefar(2, i, far_rows).start()

    cfar_copy(cmine).start()
    ccore_copy(cmine).start()
    for i in range(2):
        dcore(1, i, core_rows).wait_recv()
        dcorefar(1, i, far_core_rows).wait_recv()
    prepare(theirs)
    for k in (3, 4):
        relax_window(V1, V2, layer(k))

    @pl.when(fhigh)
    def _():
        rback(onward).wait_recv()
        dbackcore(1 - lane_of).wait_recv()
        prepare(far_slot)

    relax_window(V1, V2, layer(5))

    @pl.when(fhigh)
    def _():
        relax_window(V1, V2, layer(6))

    restrict(4 - 2 * odd, base + even)

    @pl.when(flow)
    def _():
        for i in range(2):
            dcore(2, i, core_rows).wait_recv()
            dcorefar(2, i, far_core_rows).wait_recv()
        for c in range(len(pieces)):
            rfwd(c, back).wait_recv()
        prepare(near_slot)

    relax_window(V1, V2, layer(2))

    @pl.when(flow)
    def _():
        relax_window(V1, V2, layer(1))

    restrict(2 + 2 * odd, base + odd)

    rview = lambda b: CR.at[pl.ds(b - lax.rem(b, 2), 2), coarse_rows_of(lax.rem(b, 2)), :]
    rgather = (rview, bzs, bps, br)
    gather_start(*rgather)

    def edge_copy(buf, ss, rs, d, dest):
        return remote(buf.at[2 + 3 * d], buf.at[6 - 5 * d], ss.at[d], rs.at[d], dest, j)

    def edges_start(buf, ss, rs):
        @pl.when(down)
        def _():
            edge_copy(buf, ss, rs, 0, below).start()

        @pl.when(up)
        def _():
            edge_copy(buf, ss, rs, 1, above).start()

    def edges_finish(buf, ss, rs):
        @pl.when(up)
        def _():
            edge_copy(buf, ss, rs, 0, above).wait_recv()

        @pl.when(down)
        def _():
            edge_copy(buf, ss, rs, 1, below).wait_recv()

    def edges_sent(buf, ss, rs):
        @pl.when(down)
        def _():
            edge_copy(buf, ss, rs, 0, below).wait_send()

        @pl.when(up)
        def _():
            edge_copy(buf, ss, rs, 1, above).wait_send()

    part = hy // 2
    cross = [(3, 0, part), (3, part, part), (4, 0, part), (4, part, part), (5 - 3 * odd, 0, hy), (6 - 5 * odd, 0, hy)]
    cross_in = [(3, 0, part), (3, part, part), (4, 0, part), (4, part, part), (5 - 3 * even, 0, hy), (6 - 5 * even, 0, hy)]

    def wsend(c):
        q, start, size = cross[c]
        return remote(
            W4.at[q, eight(lead + start, size), :], WX.at[q - 3 + 2 * odd, pl.ds(start, size), :], xs.at[c], xr.at[c], partner, j
        )

    def wrecv(c):
        q, start, size = cross_in[c]
        return remote(
            W4.at[q, eight(lead + start, size), :], WX.at[q - 1 - 2 * odd, pl.ds(start, size), :], xs.at[c], xr.at[c], partner, j
        )

    relax_window(V2, W3, 2)
    relax_window(V2, W3, 5)

    def third_middle(q, carry):
        relax_window(V2, W3, q)
        return carry

    lax.fori_loop(3, 5, third_middle, 0)

    def fourth_middle(q, carry):
        relax_window(W3, W4, q)
        return carry

    lax.fori_loop(3, 5, fourth_middle, 0)
    for c in range(3):
        wsend(c).start()
    cfar_copy(cfar).wait_recv()
    ccorefar_copy(cfar).start()
    gather_forward(*rgather)
    edges_start(W3, w3s, w3r)
    ccore_copy(ccore).wait_recv()
    ccorefar_copy(cfarcore).wait_recv()

    edge = hy // TILES
    lane_tile = iota((hz, hz), 0) // (hz // TILES) == iota((hz, hz), 1) // (hz // TILES)
    same_tile = lane_tile.astype(BF16)

    def lane_sums(x):
        return sum(dot(piece, same_tile) for piece in split(x, 3))

    bgf = bg_ref[...].astype(F32).astype(BF16)
    ids = []
    for ty in range(TILES):
        pick = iota((TILES * TILES, hz), 0) == ty * TILES + iota((TILES * TILES, hz), 1) // (hz // TILES)
        ids.append(dot(bgf, pick.astype(BF16)))

    brick_row = iota((n, hz), 0)
    lane = iota((n, hz), 1)
    tile_lanes = hz // TILES

    def lower_brick(x, fill):
        return jnp.where(brick_row == 0, fill, pltpu.roll(x, 1, 0))

    def upper_brick(x, fill):
        return jnp.where(brick_row == n - 1, fill, pltpu.roll(x, n - 1, 0))

    def group_sums(fields):
        out = []
        for ty in range(TILES):
            total = jnp.zeros((n, hz), F32)
            for b in range(n):
                total = total + jnp.where(ids[ty][b : b + 1] == ids[ty], fields[ty][b : b + 1], 0.0)
            out.append(total)
        return out

    def coarse_first(b, carry):
        d = DC[b]
        CI[b] = relax_fine / (d + 14.0 * kap1)
        for ty in range(TILES):
            DSUM[ty, pl.ds(b, 1), :] = jnp.sum(d[ty * edge : (ty + 1) * edge], axis=0, keepdims=True)
        return carry

    lax.fori_loop(0, n, coarse_first, 0)
    dens_sum = [lane_sums(DSUM[ty]) for ty in range(TILES)]
    weight = []
    for ty in range(TILES):
        fx = 1.0 + 0.5 * (lower_brick(ids[ty], -1.0) == ids[ty]).astype(F32)
        fx = fx + 0.5 * (upper_brick(ids[ty], -1.0) == ids[ty]).astype(F32)
        cells = edge * tile_lanes
        weight.append(16.0 * cells - 2.0 * (2 * edge - 1) * (2 * tile_lanes - 1) * fx)
    totals0 = group_sums(dens_sum)
    totals1 = group_sums(weight)
    step = [relax_coarse / (totals0[ty] + kap1 * totals1[ty]) for ty in range(TILES)]

    def invert(i, carry):
        IE[i] = relax_fine / (D[odd + i // 2, lax.rem(i, 2)] + 14.0 * kap)
        return carry

    lax.fori_loop(0, 6, invert, 0)
    edges_finish(W3, w3s, w3r)
    relax_window(W3, W4, 2)
    relax_window(W3, W4, 5)
    edges_start(W4, w4s, w4r)
    gather_finish(*rgather)
    wsend(3).start()
    wsend(4).start()

    def coarse_start(b, carry):
        CA[b + 1] = CR[b] * CI[b]
        return carry

    lax.fori_loop(0, n, coarse_start, 0)

    def coarse_defect(src, b):
        v = src[b + 1]
        f = stencil(src[b], v, src[b + 2])
        return v, CR[b] - (DC[b] + 16.0 * kap1) * v + 2.0 * kap1 * f

    def coarse_relax(src, dst):
        def body(b, carry):
            v = src[b + 1]
            f = stencil(src[b], v, src[b + 2])
            dst[b + 1] = (1.0 - relax_fine) * v + CI[b] * (CR[b] + 2.0 * kap1 * (f - v))
            return carry

        return body

    lax.fori_loop(0, n, coarse_relax(CA, CB), 0)

    def remainder(b, carry):
        defect = coarse_defect(CB, b)[1]
        for ty in range(TILES):
            RS[ty, pl.ds(b, 1), :] = jnp.sum(defect[ty * edge : (ty + 1) * edge], axis=0, keepdims=True)
        return carry

    lax.fori_loop(0, n, remainder, 0)
    group_rhs = group_sums([lane_sums(RS[ty]) for ty in range(TILES)])
    fix = [step[ty] * group_rhs[ty] for ty in range(TILES)]

    def aggregate_image(g):
        along = [x + 0.5 * (lower_brick(x, 0.0) + upper_brick(x, 0.0)) for x in g]
        blank = jnp.zeros((n, hz), F32)
        out = []
        for ty in range(TILES):
            below = along[ty - 1] if ty > 0 else blank
            above = along[ty + 1] if ty < TILES - 1 else blank
            mid = (2.0 * edge - 1.0) * along[ty] + 0.5 * (below + above)
            left = jnp.where(lane < tile_lanes, 0.0, pltpu.roll(mid, tile_lanes, 1))
            right = jnp.where(lane >= hz - tile_lanes, 0.0, pltpu.roll(mid, hz - tile_lanes, 1))
            f = (2.0 * tile_lanes - 1.0) * mid + 0.5 * (left + right)
            own = dens_sum[ty] + 16.0 * kap1 * (edge * tile_lanes)
            out.append(own * g[ty] - 2.0 * kap1 * f)
        return group_sums(out)

    for _ in range(COARSE_SWEEPS - 1):
        image = aggregate_image(fix)
        fix = [fix[ty] + step[ty] * (group_rhs[ty] - image[ty]) for ty in range(TILES)]
    for ty in range(TILES):
        FX[ty] = fix[ty]

    def add_fix(b, carry):
        for ty in range(TILES):
            part = pl.ds(ty * edge, edge)
            CA[b + 1, part, :] = CB[b + 1, part, :] + FX[ty, pl.ds(b, 1), :]
        return carry

    def near(width):
        return jnp.maximum(me - width, 0), jnp.minimum(me + width + 1, n)

    lax.fori_loop(*near(4), add_fix, 0)
    lax.fori_loop(*near(3), coarse_relax(CA, CB), 0)
    lax.fori_loop(*near(2), coarse_relax(CB, CA), 0)

    edges_finish(W4, w4s, w4r)
    wsend(5).start()

    def inside(e):
        g = 2 * me + e - 3
        return jnp.logical_and(g >= 0, g < 2 * n)

    for t in range(5):
        b = me + t - 2
        valid = jnp.logical_and(b >= 0, b < n)
        fine = jnp.where(valid, refine_layer(CA[jnp.clip(b, 0, n - 1) + 1]), 0.0)
        for e in (2 * t - 1, 2 * t):
            if 0 <= e < 8:
                S[e] = fine

    def relax_error(src, e):
        v = src[e]
        f = stencil(src[e - 1], v, src[e + 1])
        out = (1.0 - relax_fine) * v + IE[e - 1] * (2.0 * kap * (f - v))
        return jnp.where(inside(e), out, 0.0)

    def third(e, carry):
        E3[e] = relax_error(S, e)
        return carry

    lax.fori_loop(1, 7, third, 0)
    for c in range(6):
        wrecv(c).wait_recv()

    def fourth(e, carry):
        S[e] = relax_error(E3, e)
        q = e - 1 + 2 * odd
        S[e, my_half, :] = S[e, my_half, :] + W4[q, eight(lead, hy), :]
        S[e, their_half, :] = S[e, their_half, :] + WX[e - 2]
        return carry

    lax.fori_loop(2, 6, fourth, 0)

    def last(i, carry):
        v = S[i + 3]
        sol_ref[i] = v
        f = stencil(S[i + 2], v, S[i + 4])
        res_ref[i] = RF[i] - (D[mine, i] + 16.0 * kap) * v + 2.0 * kap * f
        return carry

    lax.fori_loop(0, 2, last, 0)

    for i in range(2):
        dpair(i, mine).wait_send()
    for c in range(len(pieces)):
        rpair(c, mine).wait_send()
    for kind in (0, 1):
        for i in range(2):
            dfar(kind, i, my_rows).wait_send()
            dcore(kind, i, my_rows).wait_send()
            dcorefar(kind, i, far_rows).wait_send()

    @pl.when(flow)
    def _():
        rback(back).wait_send()
        dback(back).wait_send()
        for i in range(2):
            dfar(2, i, my_rows).wait_send()
            dcore(2, i, my_rows).wait_send()
            dcorefar(2, i, far_rows).wait_send()

    @pl.when(fhigh)
    def _():
        dbackcore(lane_of).wait_send()
        for i in range(2):
            dfwd(i, onward).wait_send()
        for c in range(len(pieces)):
            rfwd(c, onward).wait_send()

    gather_sent(*dgather)
    gather_sent(*rgather)
    cfar_copy(cmine).wait_send()
    ccore_copy(cmine).wait_send()
    ccorefar_copy(cfar).wait_send()
    edges_sent(W3, w3s, w3r)
    edges_sent(W4, w4s, w4r)
    for c in range(6):
        wsend(c).wait_send()


def local(n, spec, rhs, density, kappa, block_group):
    _, cells, ny, nz = rhs.shape
    hy, hz = ny // 2, nz // 2
    window = hy + 8
    count = len(pieces_of(window))
    fine = lambda *lead: pltpu.VMEM(lead + (ny, nz), F32)
    strip = lambda *lead: pltpu.VMEM(lead + (window, nz), F32)
    coarse = lambda *lead: pltpu.VMEM(lead + (hy, hz), F32)
    dma = lambda *shape: pltpu.SemaphoreType.DMA(shape)
    vmem = pl.BlockSpec(memory_space=pltpu.VMEM)
    out = jax.ShapeDtypeStruct((cells, ny, nz), F32)
    hbm = lambda x: pltpu.with_memory_space_constraint(x, pltpu.HBM)
    sol, res = pl.pallas_call(
        functools.partial(kernel, n, spec),
        out_shape=(out, out),
        in_specs=[pl.BlockSpec(memory_space=pltpu.HBM)] * 4,
        out_specs=(vmem, vmem),
        scratch_shapes=[
            pltpu.SMEM((1,), F32), pltpu.VMEM(block_group.shape, jnp.int32),
            strip(8), fine(2), fine(4, 2), strip(8), fine(6), strip(8), strip(8), strip(8), strip(8),
            pltpu.VMEM((4, hy, nz), F32), fine(8), fine(8),
            coarse(n), coarse(n), coarse(n), coarse(n + 2), coarse(n + 2),
            pltpu.VMEM((TILES, n, hz), F32), pltpu.VMEM((TILES, n, hz), F32), pltpu.VMEM((TILES, n, hz), F32),
            dma(count), dma(count), dma(count), dma(count), dma(1), dma(1), dma(2, 2), dma(2, 2),
            dma(3, 3, 2), dma(3, 3, 2), dma(2), dma(2),
            dma(n // 2), dma(n // 2), dma(n), dma(3), dma(3),
            dma(n // 2), dma(n // 2), dma(n), dma(2), dma(2), dma(2), dma(2), dma(6), dma(6), dma(5),
        ],
        compiler_params=pltpu.CompilerParams(
            collective_id=0, has_side_effects=True, vmem_limit_bytes=(26 << 20) + 24 * n * hy * hz
        ),
    )(kappa, hbm(block_group), hbm(rhs.reshape(cells, ny, nz)), hbm(density))
    return sol[None], res[None]


def solution(mesh):
    return jax.shard_map(
        functools.partial(local, mesh.shape["brick"], mesh.shape["spec"]),
        mesh=mesh,
        in_specs=(P("spec", "brick", None, None), P("brick", "spec", None), P("spec"), P()),
        out_specs=(P("spec", "brick", None, None), P("spec", "brick", None, None)),
        check_vma=False,
    )
```

time: 49.9 us -> 48.5 us (0.972)
  Pallas kernels: 46.9 us -> 45.5 us
    pallas_call x1, Pallas kernels: 46.9 us -> 45.5 us  [local(): pl.pallas_call(functools.partial(kernel, n, spec), out_shape=(out, out),...]
where the time goes in v2:
time: 48.5 us; the launch traced here: 48.4 us
  Pallas kernels  45.5 us (94%)
  local copies, waits for them, and re-layouts  1.59 us (3%)
  between operations  1.28 us (3%)
    pallas_call x1, Pallas kernels, local(): pl.pallas_call(functools.partial(kernel, n, spec), out_shape=(out, out),...  45.5 us
    unnamed x2, local copies, waits for them, and re-layouts  1.59 us

profile of v2, /device:TPU:0, one launch (start us, length us, event | category | flops | bytes accessed | tf_op | source)
XLA Modules:
  0.0 48.4 jit_solution(12796265539253864852)
XLA Ops:
  1.3 45.5 %shard_map.59 = (f32[2,256,256]{2,1,0:T(8,128)S(1)}, f32[2,256,256]{2,1,0:T(8,128)S(1)}) custom-call(f32[1]{0:T(128)S(6)} %copy.8.kappa_hbm, s32[8,16]{1,0:T(8,128)} %bg_hbm.1, f32[2,256,256]{2,1,0:T(8,128)} %bitcast.5, f32[2,64,256]{2,1,0:T(8,128)} %dens_ref.1), custom_call_target="tpu_custom_call" | custom-call | tf_op jit(solution)/shard_map/pallas_call | solution.py:713
  46.8 0.8 %copy.9 = f32[1,2,256,256]{3,2,1,0:T(8,128)} copy(f32[1,2,256,256]{3,2,1,0:T(8,128)S(1)} %bitcast.4) | data formatting | bytes 1048576
  47.6 0.8 %copy.10 = f32[1,2,256,256]{3,2,1,0:T(8,128)} copy(f32[1,2,256,256]{3,2,1,0:T(8,128)S(1)} %bitcast.3) | data formatting | bytes 1048576

commit v3 on v2

--- a/solution.py
+++ b/solution.py
@@ -90,7 +90,7 @@
 
 
 def kernel(
-    n, spec, kappa_hbm, bg_hbm, rhs_ref, dens_ref, sol_ref, res_ref,
+    n, spec, kappa_hbm, bg_hbm, rhs_ref, dens_ref, out_ref,
     kappa_ref, bg_ref,
     R, RF, D, IW, IE, V1, V2, W3, W4, WX, S, E3, CR, DC, CI, CA, CB, RS, DSUM, FX,
     prs, prr, frs, frr, rgs, rgr, dss, dsr, gss, gsr, dgs, dgr,
@@ -266,7 +266,10 @@
         rback(back).start()
 
     gather_start(*dgather)
-    for c in range(len(pieces)):
+    dpair(0, mine).wait_send()
+    rpair(0, mine).start()
+    dpair(1, mine).wait_send()
+    for c in range(1, len(pieces)):
         rpair(c, mine).start()
 
     def cfar_copy(at):
@@ -277,18 +280,6 @@
 
     def ccorefar_copy(at):
         return remote(DC.at[:, cfar, :], DC.at[:, at, :], ass.at[2], asr.at[2], me, core)
-
-    for i in range(2):
-        dpair(i, theirs).wait_recv()
-
-        @pl.when(fhigh)
-        def _():
-            dfwd(i, onward).start()
-
-        dfar(1, i, my_rows).start()
-        dcore(1, i, my_rows).start()
-        dfar(0, i, far_rows).wait_recv()
-        dcorefar(0, i, far_rows).start()
 
     def pass_on(c):
         rpair(c, theirs).wait_recv()
@@ -296,37 +287,6 @@
         @pl.when(fhigh)
         def _():
             rfwd(c, onward).start()
-
-    for i in range(2):
-        dcore(0, i, core_rows).wait_recv()
-        dcorefar(0, i, far_core_rows).wait_recv()
-
-    @pl.when(flow)
-    def _():
-        dback(back).start()
-
-    pass_on(0)
-    pass_on(1)
-    gather_forward(*dgather)
-
-    @pl.when(flow)
-    def _():
-        for i in range(2):
-            dfwd(i, back).wait_recv()
-            dfar(2, i, my_rows).start()
-            dcore(2, i, my_rows).start()
-
-    pass_on(2)
-    for i in range(2):
-        dfar(1, i, far_rows).wait_recv()
-        dcorefar(1, i, far_rows).start()
-    for c in range(3, len(pieces)):
-        pass_on(c)
-    gather_finish(*dgather)
-    @pl.when(fhigh)
-    def _():
-        dback(onward).wait_recv()
-        dbackcore(lane_of).start()
 
     def prepare(slot):
         def body(i, carry):
@@ -357,21 +317,60 @@
     def coarse_rows_of(parity):
         return eight(parity * chalf, chalf)
 
+    def rview(side, b):
+        return CR.at[b if side else b + 1 - 2 * lax.rem(b, 2), coarse_rows_of(lax.rem(b, 2)), :]
+
+    rgathers = [(functools.partial(rview, side), bzs.at[side], bps.at[side], br.at[side]) for side in range(2)]
+
     def restrict(q, brick):
         CR[brick, coarse_rows_of(odd), :] = coarsen_sum(residual_window(q) + residual_window(q + 1), pick)
 
     loads[3].wait()
     loads[4].wait()
+    for i in range(2):
+        dpair(i, theirs).wait_recv()
+
+        @pl.when(fhigh)
+        def _():
+            dfwd(i, onward).start()
+
+        dfar(1, i, my_rows).start()
+        dcore(1, i, my_rows).start()
+        dfar(0, i, far_rows).wait_recv()
+        dcorefar(0, i, far_rows).start()
+
+    for i in range(2):
+        dcore(0, i, core_rows).wait_recv()
+        dcorefar(0, i, far_core_rows).wait_recv()
+
+    @pl.when(flow)
+    def _():
+        dback(back).start()
+
     prepare(mine)
+    pass_on(0)
 
     @pl.when(flow)
     def _():
         for i in range(2):
-            dfar(2, i, far_rows).wait_recv()
-            dcorefar(2, i, far_rows).start()
-
-    cfar_copy(cmine).start()
-    ccore_copy(cmine).start()
+            dfwd(i, back).wait_recv()
+            dfar(2, i, my_rows).start()
+            dcore(2, i, my_rows).start()
+
+    pass_on(1)
+    for i in range(2):
+        dfar(1, i, far_rows).wait_recv()
+        dcorefar(1, i, far_rows).start()
+    pass_on(2)
+    gather_forward(*dgather)
+    for c in range(3, len(pieces)):
+        pass_on(c)
+
+    @pl.when(fhigh)
+    def _():
+        dback(onward).wait_recv()
+        dbackcore(lane_of).start()
+
     for i in range(2):
         dcore(1, i, core_rows).wait_recv()
         dcorefar(1, i, far_core_rows).wait_recv()
@@ -379,6 +378,12 @@
     for k in (3, 4):
         relax_window(V1, V2, layer(k))
 
+    @pl.when(flow)
+    def _():
+        for i in range(2):
+            dfar(2, i, far_rows).wait_recv()
+            dcorefar(2, i, far_rows).start()
+
     @pl.when(fhigh)
     def _():
         rback(onward).wait_recv()
@@ -392,6 +397,10 @@
         relax_window(V1, V2, layer(6))
 
     restrict(4 - 2 * odd, base + even)
+    gather_start(*rgathers[0])
+    gather_finish(*dgather)
+    cfar_copy(cmine).start()
+    ccore_copy(cmine).start()
 
     @pl.when(flow)
     def _():
@@ -410,9 +419,7 @@
 
     restrict(2 + 2 * odd, base + odd)
 
-    rview = lambda b: CR.at[pl.ds(b - lax.rem(b, 2), 2), coarse_rows_of(lax.rem(b, 2)), :]
-    rgather = (rview, bzs, bps, br)
-    gather_start(*rgather)
+    gather_start(*rgathers[1])
 
     def edge_copy(buf, ss, rs, d, dest):
         return remote(buf.at[2 + 3 * d], buf.at[6 - 5 * d], ss.at[d], rs.at[d], dest, j)
@@ -478,7 +485,8 @@
         wsend(c).start()
     cfar_copy(cfar).wait_recv()
     ccorefar_copy(cfar).start()
-    gather_forward(*rgather)
+    for rgather in rgathers:
+        gather_forward(*rgather)
     edges_start(W3, w3s, w3r)
     ccore_copy(ccore).wait_recv()
     ccorefar_copy(cfarcore).wait_recv()
@@ -543,7 +551,8 @@
     relax_window(W3, W4, 2)
     relax_window(W3, W4, 5)
     edges_start(W4, w4s, w4r)
-    gather_finish(*rgather)
+    for rgather in rgathers:
+        gather_finish(*rgather)
     wsend(3).start()
     wsend(4).start()
 
@@ -653,15 +662,13 @@
 
     def last(i, carry):
         v = S[i + 3]
-        sol_ref[i] = v
+        out_ref[0, i] = v
         f = stencil(S[i + 2], v, S[i + 4])
-        res_ref[i] = RF[i] - (D[mine, i] + 16.0 * kap) * v + 2.0 * kap * f
+        out_ref[1, i] = RF[i] - (D[mine, i] + 16.0 * kap) * v + 2.0 * kap * f
         return carry
 
     lax.fori_loop(0, 2, last, 0)
 
-    for i in range(2):
-        dpair(i, mine).wait_send()
     for c in range(len(pieces)):
         rpair(c, mine).wait_send()
     for kind in (0, 1):
@@ -688,7 +695,8 @@
             rfwd(c, onward).wait_send()
 
     gather_sent(*dgather)
-    gather_sent(*rgather)
+    for rgather in rgathers:
+        gather_sent(*rgather)
     cfar_copy(cmine).wait_send()
     ccore_copy(cmine).wait_send()
     ccorefar_copy(cfar).wait_send()
@@ -708,13 +716,13 @@
     coarse = lambda *lead: pltpu.VMEM(lead + (hy, hz), F32)
     dma = lambda *shape: pltpu.SemaphoreType.DMA(shape)
     vmem = pl.BlockSpec(memory_space=pltpu.VMEM)
-    out = jax.ShapeDtypeStruct((cells, ny, nz), F32)
+    out = jax.ShapeDtypeStruct((2, cells, ny, nz), F32)
     hbm = lambda x: pltpu.with_memory_space_constraint(x, pltpu.HBM)
-    sol, res = pl.pallas_call(
+    both = pl.pallas_call(
         functools.partial(kernel, n, spec),
-        out_shape=(out, out),
+        out_shape=out,
         in_specs=[pl.BlockSpec(memory_space=pltpu.HBM)] * 4,
-        out_specs=(vmem, vmem),
+        out_specs=vmem,
         scratch_shapes=[
             pltpu.SMEM((1,), F32), pltpu.VMEM(block_group.shape, jnp.int32),
             strip(8), fine(2), fine(4, 2), strip(8), fine(6), strip(8), strip(8), strip(8), strip(8),
@@ -724,13 +732,13 @@
             dma(count), dma(count), dma(count), dma(count), dma(1), dma(1), dma(2, 2), dma(2, 2),
             dma(3, 3, 2), dma(3, 3, 2), dma(2), dma(2),
             dma(n // 2), dma(n // 2), dma(n), dma(3), dma(3),
-            dma(n // 2), dma(n // 2), dma(n), dma(2), dma(2), dma(2), dma(2), dma(6), dma(6), dma(5),
+            dma(2, n // 2), dma(2, n // 2), dma(2, n), dma(2), dma(2), dma(2), dma(2), dma(6), dma(6), dma(5),
         ],
         compiler_params=pltpu.CompilerParams(
             collective_id=0, has_side_effects=True, vmem_limit_bytes=(26 << 20) + 24 * n * hy * hz
         ),
     )(kappa, hbm(block_group), hbm(rhs.reshape(cells, ny, nz)), hbm(density))
-    return sol[None], res[None]
+    return both[:1], both[1:]
 
 
 def solution(mesh):

time: 48.5 us -> 46.4 us (0.957)
  Pallas kernels: 45.5 us -> 43.9 us
  local copies, waits for them, and re-layouts: 1.59 us -> 1.03 us
    unnamed x2 -> x0, local copies, waits for them, and re-layouts: 1.59 us -> none
    pallas_call x1, Pallas kernels: 45.5 us -> 43.9 us  [local(): pl.pallas_call(functools.partial(kernel, n, spec), out_shape=out, in_spec...]
    slice x0 -> x1, local copies, waits for them, and re-layouts: none -> 1.03 us  [local(): return (both[:1], both[1:])]
where the time goes in v3:
time: 46.4 us; the launch traced here: 46.2 us
  Pallas kernels  43.9 us (95%)
  between operations  1.28 us (3%)
  local copies, waits for them, and re-layouts  1.03 us (2%)
    pallas_call x1, Pallas kernels, local(): pl.pallas_call(functools.partial(kernel, n, spec), out_shape=out, in_spec...  43.9 us
    slice x1, local copies, waits for them, and re-layouts, local(): return (both[:1], both[1:])  1.03 us

profile of v3, /device:TPU:0, one launch (start us, length us, event | category | flops | bytes accessed | tf_op | source)
XLA Modules:
  0.0 46.2 jit_solution(8336062779675463774)
XLA Ops:
  1.3 43.9 %shard_map.59 = f32[2,2,256,256]{3,2,1,0:T(8,128)S(1)} custom-call(f32[1]{0:T(128)S(6)} %copy.6.kappa_hbm, s32[8,16]{1,0:T(8,128)} %bg_hbm.1, f32[2,256,256]{2,1,0:T(8,128)} %bitcast.1, f32[2,64,256]{2,1,0:T(8,128)} %dens_ref.1), custom_call_target="tpu_custom_call" | custom-call | tf_op jit(solution)/shard_map/pallas_call | solution.py:721
  45.2 1.0 %fusion = (f32[1,2,256,256]{3,2,1,0:T(8,128)}, f32[1,2,256,256]{3,2,1,0:T(8,128)}) fusion(f32[2,2,256,256]{3,2,1,0:T(8,128)S(1)} %shard_map.59), kind=kLoop, calls=%fused_computation | loop fusion | bytes 2097152 | tf_op jit(solution)/shard_map/slice | solution.py:741

commit v4 on v3

--- a/solution.py
+++ b/solution.py
@@ -165,6 +165,10 @@
         for buf, q in ((V1, 6), (V1, 7), (V2, 6), (W3, 6), (W4, 6)):
             buf[q] = blank
 
+    @pl.when(jnp.logical_not(flow))
+    def _():
+        WX[3 * odd] = jnp.zeros((hy, nz), F32)
+
     zero = jnp.zeros((hy, hz), F32)
     for buf in (CA, CB):
         buf[0] = zero
@@ -623,7 +627,10 @@
     lax.fori_loop(*near(2), coarse_relax(CB, CA), 0)
 
     edges_finish(W4, w4s, w4r)
-    wsend(5).start()
+
+    @pl.when(fhigh)
+    def _():
+        wsend(5).start()
 
     def inside(e):
         g = 2 * me + e - 3
@@ -648,8 +655,12 @@
         return carry
 
     lax.fori_loop(1, 7, third, 0)
-    for c in range(6):
+    for c in range(5):
         wrecv(c).wait_recv()
+
+    @pl.when(flow)
+    def _():
+        wrecv(5).wait_recv()
 
     def fourth(e, carry):
         S[e] = relax_error(E3, e)
@@ -702,8 +713,12 @@
     ccorefar_copy(cfar).wait_send()
     edges_sent(W3, w3s, w3r)
     edges_sent(W4, w4s, w4r)
-    for c in range(6):
+    for c in range(5):
         wsend(c).wait_send()
+
+    @pl.when(fhigh)
+    def _():
+        wsend(5).wait_send()
 
 
 def local(n, spec, rhs, density, kappa, block_group):

time: 46.4 us -> 44.6 us (0.961); the launches traced: 46.2 us -> 43.9 us
  Pallas kernels: 43.9 us -> 41.6 us
    pallas_call x1, Pallas kernels: 43.9 us -> 41.6 us  [local(): pl.pallas_call(functools.partial(kernel, n, spec), out_shape=out, in_spec...]
where the time goes in v4:
time: 44.6 us; the launch traced here: 43.9 us
  Pallas kernels  41.6 us (93%)
  between operations  1.28 us (3%)
  local copies, waits for them, and re-layouts  1.03 us (2%)
    pallas_call x1, Pallas kernels, local(): pl.pallas_call(functools.partial(kernel, n, spec), out_shape=out, in_spec...  41.6 us
    slice x1, local copies, waits for them, and re-layouts, local(): return (both[:1], both[1:])  1.03 us

profile of v4, /device:TPU:0, one launch (start us, length us, event | category | flops | bytes accessed | tf_op | source)
XLA Modules:
  0.0 43.9 jit_solution(2248110195437490272)
XLA Ops:
  1.3 41.6 %shard_map.59 = f32[2,2,256,256]{3,2,1,0:T(8,128)S(1)} custom-call(f32[1]{0:T(128)S(6)} %copy.6.kappa_hbm, s32[8,16]{1,0:T(8,128)} %bg_hbm.1, f32[2,256,256]{2,1,0:T(8,128)} %bitcast.1, f32[2,64,256]{2,1,0:T(8,128)} %dens_ref.1), custom_call_target="tpu_custom_call" | custom-call | tf_op jit(solution)/shard_map/pallas_call | solution.py:736
  42.9 1.0 %fusion = (f32[1,2,256,256]{3,2,1,0:T(8,128)}, f32[1,2,256,256]{3,2,1,0:T(8,128)}) fusion(f32[2,2,256,256]{3,2,1,0:T(8,128)S(1)} %shard_map.59), kind=kLoop, calls=%fused_computation | loop fusion | bytes 2097152 | tf_op jit(solution)/shard_map/slice | solution.py:756

commit v5 on v4

--- a/solution.py
+++ b/solution.py
@@ -487,10 +487,10 @@
     lax.fori_loop(3, 5, fourth_middle, 0)
     for c in range(3):
         wsend(c).start()
+    gather_forward(*rgathers[0])
     cfar_copy(cfar).wait_recv()
     ccorefar_copy(cfar).start()
-    for rgather in rgathers:
-        gather_forward(*rgather)
+    gather_forward(*rgathers[1])
     edges_start(W3, w3s, w3r)
     ccore_copy(ccore).wait_recv()
     ccorefar_copy(cfarcore).wait_recv()
@@ -580,7 +580,7 @@
 
         return body
 
-    lax.fori_loop(0, n, coarse_relax(CA, CB), 0)
+    lax.fori_loop(0, n, coarse_relax(CA, CB), 0, unroll=2)
 
     def remainder(b, carry):
         defect = coarse_defect(CB, b)[1]
@@ -588,7 +588,7 @@
             RS[ty, pl.ds(b, 1), :] = jnp.sum(defect[ty * edge : (ty + 1) * edge], axis=0, keepdims=True)
         return carry
 
-    lax.fori_loop(0, n, remainder, 0)
+    lax.fori_loop(0, n, remainder, 0, unroll=2)
     group_rhs = group_sums([lane_sums(RS[ty]) for ty in range(TILES)])
     fix = [step[ty] * group_rhs[ty] for ty in range(TILES)]
 
@@ -654,22 +654,27 @@
         E3[e] = relax_error(S, e)
         return carry
 
-    lax.fori_loop(1, 7, third, 0)
-    for c in range(5):
-        wrecv(c).wait_recv()
-
-    @pl.when(flow)
-    def _():
-        wrecv(5).wait_recv()
+    lax.fori_loop(1, 7, third, 0, unroll=2)
 
     def fourth(e, carry):
         S[e] = relax_error(E3, e)
         q = e - 1 + 2 * odd
         S[e, my_half, :] = S[e, my_half, :] + W4[q, eight(lead, hy), :]
+        return carry
+
+    lax.fori_loop(2, 6, fourth, 0)
+    for c in range(5):
+        wrecv(c).wait_recv()
+
+    @pl.when(flow)
+    def _():
+        wrecv(5).wait_recv()
+
+    def join(e, carry):
         S[e, their_half, :] = S[e, their_half, :] + WX[e - 2]
         return carry
 
-    lax.fori_loop(2, 6, fourth, 0)
+    lax.fori_loop(2, 6, join, 0)
 
     def last(i, carry):
         v = S[i + 3]

time: 44.6 us -> 43.6 us (0.978)
  Pallas kernels: 41.6 us -> 40.7 us
    pallas_call x1, Pallas kernels: 41.6 us -> 40.7 us  [local(): pl.pallas_call(functools.partial(kernel, n, spec), out_shape=out, in_spec...]
where the time goes in v5:
time: 43.6 us; the launch traced here: 43 us
  Pallas kernels  40.7 us (93%)
  between operations  1.28 us (3%)
  local copies, waits for them, and re-layouts  1.03 us (2%)
    pallas_call x1, Pallas kernels, local(): pl.pallas_call(functools.partial(kernel, n, spec), out_shape=out, in_spec...  40.7 us
    slice x1, local copies, waits for them, and re-layouts, local(): return (both[:1], both[1:])  1.03 us

profile of v5, /device:TPU:0, one launch (start us, length us, event | category | flops | bytes accessed | tf_op | source)
XLA Modules:
  0.0 43.0 jit_solution(2946318321825695343)
XLA Ops:
  1.3 40.7 %shard_map.59 = f32[2,2,256,256]{3,2,1,0:T(8,128)S(1)} custom-call(f32[1]{0:T(128)S(6)} %copy.6.kappa_hbm, s32[8,16]{1,0:T(8,128)} %bg_hbm.1, f32[2,256,256]{2,1,0:T(8,128)} %bitcast.1, f32[2,64,256]{2,1,0:T(8,128)} %dens_ref.1), custom_call_target="tpu_custom_call" | custom-call | tf_op jit(solution)/shard_map/pallas_call | solution.py:741
  42.0 1.0 %fusion = (f32[1,2,256,256]{3,2,1,0:T(8,128)}, f32[1,2,256,256]{3,2,1,0:T(8,128)}) fusion(f32[2,2,256,256]{3,2,1,0:T(8,128)S(1)} %shard_map.59), kind=kLoop, calls=%fused_computation | loop fusion | bytes 2097152 | tf_op jit(solution)/shard_map/slice | solution.py:761

commit v6 on v5

--- a/solution.py
+++ b/solution.py
@@ -488,10 +488,10 @@
     for c in range(3):
         wsend(c).start()
     gather_forward(*rgathers[0])
+    edges_start(W3, w3s, w3r)
     cfar_copy(cfar).wait_recv()
     ccorefar_copy(cfar).start()
     gather_forward(*rgathers[1])
-    edges_start(W3, w3s, w3r)
     ccore_copy(ccore).wait_recv()
     ccorefar_copy(cfarcore).wait_recv()
 

time: 43.6 us -> 43.3 us (level)
  no operation moved by 1% of the time
where the time goes in v6:
time: 43.3 us; the launch traced here: 43 us
  Pallas kernels  40.6 us (94%)
  between operations  1.28 us (3%)
  local copies, waits for them, and re-layouts  1.03 us (2%)
    pallas_call x1, Pallas kernels, local(): pl.pallas_call(functools.partial(kernel, n, spec), out_shape=out, in_spec...  40.6 us
    slice x1, local copies, waits for them, and re-layouts, local(): return (both[:1], both[1:])  1.03 us

profile of v6, /device:TPU:0, one launch (start us, length us, event | category | flops | bytes accessed | tf_op | source)
XLA Modules:
  0.0 43.0 jit_solution(1069338775376389508)
XLA Ops:
  1.3 40.6 %shard_map.59 = f32[2,2,256,256]{3,2,1,0:T(8,128)S(1)} custom-call(f32[1]{0:T(128)S(6)} %copy.6.kappa_hbm, s32[8,16]{1,0:T(8,128)} %bg_hbm.1, f32[2,256,256]{2,1,0:T(8,128)} %bitcast.1, f32[2,64,256]{2,1,0:T(8,128)} %dens_ref.1), custom_call_target="tpu_custom_call" | custom-call | tf_op jit(solution)/shard_map/pallas_call | solution.py:741
  41.9 1.0 %fusion = (f32[1,2,256,256]{3,2,1,0:T(8,128)}, f32[1,2,256,256]{3,2,1,0:T(8,128)}) fusion(f32[2,2,256,256]{3,2,1,0:T(8,128)S(1)} %shard_map.59), kind=kLoop, calls=%fused_computation | loop fusion | bytes 2097152 | tf_op jit(solution)/shard_map/slice | solution.py:761
